TPU v7x, 32 devices: a whole 2x2x4 slice. The times are simulated.
32 devices in a mesh: grp: 2 (over y), dp: 16 (over z, x, core).
Axes of the slice: x: 2, y: 2, z: 4, core: 2. Of those that a mesh axis runs over, the one named last changes fastest.
Arguments:
- teacher_states: bfloat16 [2, 4096, 6144], P(None, 'dp', 'grp'), may hold values from -18.5 to 18.5
- student_features: bfloat16 [2, 4096, 1024], P(None, 'dp'), may hold values from -13 to 13
- w_first: bfloat16 [1024, 1024], replicated, may hold values from -0.1875 to 0.1875
- w_second: bfloat16 [1024, 1024], replicated, may hold values from -0.1875 to 0.1875
Outputs:
- correlation: float32 [1024, 6144], P('dp', 'grp')
All inputs are finite; a program needn't handle non-finite values.
Results may differ from a plain program's by a relative error of at most 0.0003.
Values may be sent and summed in bfloat16 or wider, within the bound.
No kernel may reach another device: no remote copies, remote signals or barrier semaphores. Data moves between devices by JAX's collectives and lax.ppermute only.
A program may use at most 128 MiB of HBM per device.

v0:
```python
import math
import jax
import jax.numpy as jnp
from jax import lax
from jax.sharding import PartitionSpec as P

DT = 6144
EPSILON = 1e-06


def normalize_rows(states):
    values = states.astype(jnp.float32)
    sums = (jnp.sum(values, axis=1), jnp.sum(values * values, axis=1))
    totals = lax.psum((sums[0], sums[1]), "grp")
    row_mean = totals[0] / DT
    row_var = totals[1] / DT - row_mean * row_mean
    return (values - row_mean[:, None]) * lax.rsqrt(row_var + EPSILON)[:, None]


def teacher_side(states, token_total):
    normed = normalize_rows(states)
    power = lax.psum(jnp.sum(normed * normed, axis=0), "dp")
    return (normed * lax.rsqrt(power / token_total + EPSILON)).astype(jnp.bfloat16)


def project(features, w_first, w_second):
    hidden = jax.nn.gelu(jnp.dot(features, w_first, preferred_element_type=jnp.float32)).astype(
        jnp.bfloat16
    )
    return jnp.dot(hidden, w_second, preferred_element_type=jnp.float32)


def column_sums(projected):
    sums = (jnp.sum(projected, axis=0), jnp.sum(projected * projected, axis=0))
    return lax.psum((sums[0], sums[1]), "dp")


def standardize(projected, totals, token_total):
    col_mean = totals[0] / token_total
    col_var = totals[1] / token_total - col_mean * col_mean
    return ((projected - col_mean) * lax.rsqrt(col_var + EPSILON)).astype(jnp.bfloat16)


def student_side(features, w_first, w_second, token_total):
    projected = project(features, w_first, w_second)
    return standardize(projected, column_sums(projected), token_total)


def make_product(pair_list):
    running = None
    for student_z, teacher_z in pair_list:
        product = lax.dot_general(
            student_z, teacher_z, (((0,), (0,)), ((), ())), preferred_element_type=jnp.float32
        )
        running = product
    return running


def shards(teacher_states, student_features, w_first, w_second):
    micro_count = teacher_states.shape[0]
    token_total = teacher_states.shape[1] * lax.axis_size("dp")
    correlation = None
    for batch_index in range(micro_count):
        teacher_z = teacher_side(teacher_states[batch_index], token_total)
        student_z = student_side(student_features[batch_index], w_first, w_second, token_total)
        portion_sum = lax.psum_scatter(
            make_product([(student_z, teacher_z)]), "dp", scatter_dimension=0, tiled=True
        )
        correlation = portion_sum if correlation is None else correlation + portion_sum
    return correlation * (1.0 / math.sqrt(micro_count * token_total))


def solution(mesh):
    placed = (P(None, "dp", "grp"), P(None, "dp", None), P(), P())
    return jax.shard_map(
        shards, mesh=mesh, in_specs=placed, out_specs=P("dp", "grp"), check_vma=False
    )
```

profile of v0, /device:TPU:0, one launch (start us, length us, event | category | flops | bytes accessed | tf_op | source)
XLA Modules:
  0.0 245.8 jit_solution(2058709502384886520)
XLA Ops:
  6.5 0.0 copy-start
  6.5 0.0 reduce-scatter.2.cloned.1.call-start
  6.5 1.9 fusion.15
  8.5 2.4 convert_reduce_fusion
  10.9 0.0 copy-done
  10.9 3.3 %fusion.83 = (f32[1024]{0:T(1024)S(1)}, f32[1024]{0:T(1024)S(1)}, f32[256,1024]{1,0:T(8,128)S(1)}) fusion(bf16[1024,1024]{1,0:T(8,128)(2,1)S(1)} %copy-done, bf16[1024,1024]{1,0:T(8,128)(2,1)} %param.6, bf16[2,256,1024]{2,1,0:T(8,128)(2,1)} %param.5), kind=kOutput, calls=%fused_computation.91 | convolution fusion | flops 1076885504 | bytes 5775360 | tf_op jit(solution)/shard_map/dot_general | solution.py:30
  14.1 4.2 %fusion.84 = (f32[1024]{0:T(1024)S(1)}, f32[1024]{0:T(1024)S(1)}, f32[256,1024]{1,0:T(8,128)}) fusion(bf16[1024,1024]{1,0:T(8,128)(2,1)S(1)} %copy-done, bf16[1024,1024]{1,0:T(8,128)(2,1)} %param.6, bf16[2,256,1024]{2,1,0:T(8,128)(2,1)} %param.5), kind=kOutput, calls=%fused_computation.92 | convolution fusion | flops 1076885504 | bytes 5775360 | tf_op jit(solution)/shard_map/dot_general | solution.py:30
  18.4 5.9 %all-reduce.2 = (f32[256]{0:T(256)S(1)}, f32[256]{0:T(256)S(1)}) all-reduce(f32[256]{0:T(256)S(1)} %fusion.15, f32[256]{0:T(256)S(1)} %get-tuple-element.7), channel_id=1, replica_groups=mesh['grp'=2,'dp'=16] {'grp'}, use_global_device_ids=true, to_apply=%region_18.0 | all-reduce | flops 512 | bytes 4096 | tf_op jit(solution)/shard_map/psum | solution.py:14
  24.2 2.8 %fusion.13 = (f32[3072]{0:T(1024)S(1)}, f32[256]{0:T(256)S(1)}) fusion(f32[256]{0:T(256)S(1)} %get-tuple-element.30, f32[256]{0:T(256)S(1)} %get-tuple-element.29, bf16[2,256,3072]{2,1,0:T(8,128)(2,1)} %param.4), kind=kLoop, calls=%fused_computation.18 | loop fusion | flops 6288128 | bytes 3161088 | tf_op jit(solution)/shard_map/reduce_sum | solution.py:22
  27.1 4.9 %all-reduce.1 = (f32[256]{0:T(256)S(1)}, f32[256]{0:T(256)S(1)}) all-reduce(f32[256]{0:T(256)S(1)} %get-tuple-element.6, f32[256]{0:T(256)S(1)} %get-tuple-element.8), channel_id=1, replica_groups=mesh['grp'=2,'dp'=16] {'grp'}, use_global_device_ids=true, to_apply=%region_7.0 | all-reduce | flops 512 | bytes 4096 | tf_op jit(solution)/shard_map/psum | solution.py:14
  32.0 2.1 fusion.7
  34.1 59.7 %all-reduce = (f32[3072]{0:T(1024)S(1)}, f32[1024]{0:T(1024)S(1)}, f32[1024]{0:T(1024)S(1)}, f32[3072]{0:T(1024)S(1)}, f32[1024]{0:T(1024)S(1)}, /*index=5*/f32[1024]{0:T(1024)S(1)}) all-reduce(f32[3072]{0:T(1024)S(1)} %fusion.7, f32[1024]{0:T(1024)S(1)} %get-tuple-element.12, ...), channel_id=1, replica_groups=mesh['grp'=2,'dp'=16] {'dp'}, use_global_device_ids=true, to_apply=%region_9.0 | all-reduce | flops 10240 | bytes 81920 | tf_op jit(solution)/shard_map/psum | solution.py:22
  93.8 0.0 copy-start.1
  93.8 3.9 %fusion.17 = f32[1024,3072]{1,0:T(8,128)S(1)} fusion(f32[3072]{0:T(1024)S(1)} %get-tuple-element.34, f32[256]{0:T(256)S(1)} %get-tuple-element.28, f32[256]{0:T(256)S(1)} %get-tuple-element.27, bf16[2,256,3072]{2,1,0:T(8,128)(2,1)} %param.4, f32[256,1024]{1,0:T(8,128)} %get-tuple-element.31, f32[1024]{0:T(1024)S(1)} %get-tuple-element.35, ...), kind=kOutput, calls=%fused_computation.21 | convolution fusion | flops 1615331328 | bytes 15226880 | tf_op jit(solution)/shard_map/dot_general | solution.py:52
  97.7 0.0 copy-done.1
  97.8 6.7 %convolution_add_fusion = f32[1024,3072]{1,0:T(8,128)} fusion(f32[1024,3072]{1,0:T(8,128)S(1)} %fusion.17, f32[3072]{0:T(1024)S(1)} %get-tuple-element.33, f32[256]{0:T(256)S(1)} %get-tuple-element.30, f32[256]{0:T(256)S(1)} %get-tuple-element.29, bf16[2,256,3072]{2,1,0:T(8,128)(2,1)S(1)} %copy-done.1, f32[256,1024]{1,0:T(8,128)S(1)} %get-tuple-element.32, ...), kind=kOutput, calls=%fused_computation | convolution fusion | flops 1618477056 | bytes 27809792 | tf_op jit(solution)/shard_map/dot_general | solution.py:52
  104.5 0.0 reduce-scatter.2.cloned.1.call-update
  104.5 132.4 %reduce-scatter.2.cloned.1.call-done = f32[64,3072]{1,0:T(8,128)} async-done(((f32[1024,3072]{1,0:T(8,128)}), f32[64,3072]{1,0:T(8,128)}) %reduce-scatter.2.cloned.1.call-update) | async-done | bytes 786448 | tf_op jit(solution)/shard_map/reduce_scatter | solution.py:66
  236.9 2.1 broadcast_multiply_fusion
  (4 shorter events, 0.0 us)
Async XLA Ops:
  6.5 4.3 %copy-start = (bf16[1024,1024]{1,0:T(8,128)(2,1)S(1)}, bf16[1024,1024]{1,0:T(8,128)(2,1)}, u32[]{:S(2)}) copy-start(bf16[1024,1024]{1,0:T(8,128)(2,1)} %param.7) | copy-start | bytes 6291460
  6.5 230.4 %reduce-scatter.2.cloned.1.call-start = ((), (), s32[]{:S(2)}) async-start(), calls=%async_computation.1 | async-start | bytes 13369344 | tf_op jit(solution)/shard_map/reduce_scatter | solution.py:66
  93.8 3.9 %copy-start.1 = (bf16[2,256,3072]{2,1,0:T(8,128)(2,1)S(1)}, bf16[2,256,3072]{2,1,0:T(8,128)(2,1)}, u32[]{:S(2)}) copy-start(bf16[2,256,3072]{2,1,0:T(8,128)(2,1)} %param.4) | copy-start | bytes 9437188
Sparse Core Ops, SparseCore 0:
  104.6 132.2 reduce-scatter.1
where the time goes:
time: 246 us
  waiting for transfers between devices  132 us (54%)
  blocking collectives  70.5 us (29%)
  matrix products  18.1 us (7%)
  between operations  13.4 us (5%)
  other arithmetic  11.4 us (5%)
    reduce_scatter x1, waiting for transfers between devices, shards(): lax.psum_scatter(make_product([(student_z, teacher_z)]), 'dp', scatter_di...  132 us
    psum x1, blocking collectives, teacher_side(): power = lax.psum(jnp.sum(normed * normed, axis=0), 'dp')  59.7 us
    psum x2, blocking collectives, normalize_rows(): totals = lax.psum((sums[0], sums[1]), 'grp')  10.8 us
    dot_general x2, matrix products, make_product(): lax.dot_general(student_z, teacher_z, (((0,), (0,)), ((), ())), preferred...  10.6 us
    dot_general x2, matrix products, project(): return jnp.dot(hidden, w_second, preferred_element_type=jnp.float32)  7.49 us
    reduce_sum x2, other arithmetic, teacher_side(): power = lax.psum(jnp.sum(normed * normed, axis=0), 'dp')  4.93 us
  transfers between devices with their start and end apart: 1, of which 1 were waited for; matrix products, arithmetic and copies ran while one was open for 0% of the time, Pallas kernels for 0%

commit v1 on v0

--- a/solution.py
+++ b/solution.py
@@ -19,7 +19,9 @@
 
 def teacher_side(states, token_total):
     normed = normalize_rows(states)
-    power = lax.psum(jnp.sum(normed * normed, axis=0), "dp")
+    block = jnp.sum(normed * normed, axis=0)
+    pieces = lax.all_gather(block, "dp")
+    power = jnp.sum(pieces, axis=0)
     return (normed * lax.rsqrt(power / token_total + EPSILON)).astype(jnp.bfloat16)
 
 

time: 246 us -> 288 us (1.17)
  blocking collectives: 70.5 us -> 111 us
    all_gather x0 -> x2, blocking collectives: none -> 40.6 us  [teacher_side(): pieces = lax.all_gather(block, 'dp')]
where the time goes in v1:
time: 288 us
  waiting for transfers between devices  132 us (46%)
  blocking collectives  111 us (39%)
  matrix products  19.4 us (7%)
  between operations  13.5 us (5%)
  other arithmetic  11.4 us (4%)
    reduce_scatter x1, waiting for transfers between devices, shards(): lax.psum_scatter(make_product([(student_z, teacher_z)]), 'dp', scatter_di...  132 us
    psum x1, blocking collectives, column_sums(): return lax.psum((sums[0], sums[1]), 'dp')  59.1 us
    all_gather x2, blocking collectives, teacher_side(): pieces = lax.all_gather(block, 'dp')  40.6 us
    psum x2, blocking collectives, normalize_rows(): totals = lax.psum((sums[0], sums[1]), 'grp')  10.8 us
    dot_general x2, matrix products, make_product(): lax.dot_general(student_z, teacher_z, (((0,), (0,)), ((), ())), preferred...  10.7 us
    dot_general x2, matrix products, project(): return jnp.dot(hidden, w_second, preferred_element_type=jnp.float32)  8.67 us
  transfers between devices with their start and end apart: 1, of which 1 were waited for; matrix products, arithmetic and copies ran while one was open for 0% of the time, Pallas kernels for 0%

profile of v1, /device:TPU:0, one launch (start us, length us, event | category | flops | bytes accessed | tf_op | source)
XLA Modules:
  0.0 287.9 jit_solution(8588649382847250513)
XLA Ops:
  6.5 0.0 copy-start
  6.5 0.0 reduce-scatter.2.cloned.1.call-start
  6.5 1.9 fusion.15
  8.5 2.4 convert_reduce_fusion
  10.9 0.0 copy-done
  10.9 3.8 %fusion.83 = (f32[1024]{0:T(1024)}, f32[1024]{0:T(1024)}, f32[256,1024]{1,0:T(8,128)S(1)}) fusion(bf16[1024,1024]{1,0:T(8,128)(2,1)S(1)} %copy-done, bf16[1024,1024]{1,0:T(8,128)(2,1)} %param.6, bf16[2,256,1024]{2,1,0:T(8,128)(2,1)} %param.5), kind=kOutput, calls=%fused_computation.91 | convolution fusion | flops 1076885504 | bytes 5775360 | tf_op jit(solution)/shard_map/dot_general | solution.py:32
  14.7 4.8 %fusion.84 = (f32[1024]{0:T(1024)}, f32[1024]{0:T(1024)}, f32[256,1024]{1,0:T(8,128)}) fusion(bf16[1024,1024]{1,0:T(8,128)(2,1)S(1)} %copy-done, bf16[1024,1024]{1,0:T(8,128)(2,1)} %param.6, bf16[2,256,1024]{2,1,0:T(8,128)(2,1)} %param.5), kind=kOutput, calls=%fused_computation.92 | convolution fusion | flops 1076885504 | bytes 5775360 | tf_op jit(solution)/shard_map/dot_general | solution.py:32
  19.5 5.9 %all-reduce.2 = (f32[256]{0:T(256)S(1)}, f32[256]{0:T(256)S(1)}) all-reduce(f32[256]{0:T(256)S(1)} %fusion.15, f32[256]{0:T(256)S(1)} %get-tuple-element.7), channel_id=1, replica_groups=mesh['grp'=2,'dp'=16] {'grp'}, use_global_device_ids=true, to_apply=%region_18.0 | all-reduce | flops 512 | bytes 4096 | tf_op jit(solution)/shard_map/psum | solution.py:14
  25.4 0.0 copy-start.2
  25.4 2.8 fusion.13
  28.2 4.9 %all-reduce.1 = (f32[256]{0:T(256)S(1)}, f32[256]{0:T(256)S(1)}) all-reduce(f32[256]{0:T(256)S(1)} %get-tuple-element.6, f32[256]{0:T(256)S(1)} %get-tuple-element.8), channel_id=1, replica_groups=mesh['grp'=2,'dp'=16] {'grp'}, use_global_device_ids=true, to_apply=%region_7.0 | all-reduce | flops 512 | bytes 4096 | tf_op jit(solution)/shard_map/psum | solution.py:14
  33.2 0.0 copy-start.4
  33.2 0.0 copy-start.5
  33.2 0.0 copy-done.2
  33.2 0.6 copy-done.4
  33.8 0.0 copy-done.5
  33.8 2.1 fusion.7
  35.9 22.7 %all-gather = f32[49152]{0:T(1024)S(1)} all-gather(f32[3072]{0:T(1024)S(1)} %fusion.7), channel_id=2, replica_groups=mesh['grp'=2,'dp'=16] {'dp'}, dimensions={0}, use_global_device_ids=true | all-gather | bytes 208896 | tf_op jit(solution)/shard_map/all_gather | solution.py:23
  58.6 18.0 %all-gather.1 = f32[49152]{0:T(1024)S(1)} all-gather(f32[3072]{0:T(1024)S(1)} %get-tuple-element.5), channel_id=3, replica_groups=mesh['grp'=2,'dp'=16] {'dp'}, dimensions={0}, use_global_device_ids=true | all-gather | bytes 208896 | tf_op jit(solution)/shard_map/all_gather | solution.py:23
  76.7 59.1 %all-reduce = (f32[1024]{0:T(1024)S(1)}, f32[1024]{0:T(1024)S(1)}, f32[1024]{0:T(1024)S(1)}, f32[1024]{0:T(1024)S(1)}) all-reduce(f32[1024]{0:T(1024)} %get-tuple-element.12, f32[1024]{0:T(1024)} %get-tuple-element.11, f32[1024]{0:T(1024)} %get-tuple-element.10, f32[1024]{0:T(1024)} %get-tuple-element.9), channel_id=1, replica_groups=mesh['grp'=2,'dp'=16] {'dp'}, use_global_device_ids=true, to_apply=%region_3.0 | all-reduce | flops 4096 | bytes 32768 | tf_op jit(solution)/shard_map/psum | solution.py:37
  135.8 0.0 copy-start.1
  135.8 0.0 copy-start.3
  135.9 3.9 %fusion.17 = f32[1024,3072]{1,0:T(8,128)S(1)} fusion(f32[3072]{0:T(1024)S(1)} %add_rsqrt_fusion.1, f32[256]{0:T(256)} %copy-done.5, f32[256]{0:T(256)} %copy-done.4, bf16[2,256,3072]{2,1,0:T(8,128)(2,1)} %param.4, f32[256,1024]{1,0:T(8,128)} %get-tuple-element.29, f32[1024]{0:T(1024)S(1)} %get-tuple-element.24, f32[1024]{0:T(1024)S(1)} %get-tuple-element.23), kind=kOutput, calls=%fused_computation.21 | convolution fusion | flops 1615331328 | bytes 15226880 | tf_op jit(solution)/shard_map/dot_general | solution.py:54
  139.8 0.0 copy-done.1
  139.8 0.0 copy-done.3
  139.8 6.8 %convolution_add_fusion = f32[1024,3072]{1,0:T(8,128)} fusion(f32[1024,3072]{1,0:T(8,128)S(1)} %fusion.17, f32[3072]{0:T(1024)S(1)} %add_rsqrt_fusion, f32[256]{0:T(256)S(1)} %copy-done.3, f32[256]{0:T(256)S(1)} %get-tuple-element.27, bf16[2,256,3072]{2,1,0:T(8,128)(2,1)S(1)} %copy-done.1, f32[256,1024]{1,0:T(8,128)S(1)} %get-tuple-element.30, ...), kind=kOutput, calls=%fused_computation | convolution fusion | flops 1618477056 | bytes 27809792 | tf_op jit(solution)/shard_map/dot_general | solution.py:54
  146.6 0.0 reduce-scatter.2.cloned.1.call-update
  146.6 132.4 %reduce-scatter.2.cloned.1.call-done = f32[64,3072]{1,0:T(8,128)} async-done(((f32[1024,3072]{1,0:T(8,128)}), f32[64,3072]{1,0:T(8,128)}) %reduce-scatter.2.cloned.1.call-update) | async-done | bytes 786448 | tf_op jit(solution)/shard_map/reduce_scatter | solution.py:68
  279.0 2.1 broadcast_multiply_fusion
  (10 shorter events, 0.2 us)
Async XLA Ops:
  6.5 4.3 %copy-start = (bf16[1024,1024]{1,0:T(8,128)(2,1)S(1)}, bf16[1024,1024]{1,0:T(8,128)(2,1)}, u32[]{:S(2)}) copy-start(bf16[1024,1024]{1,0:T(8,128)(2,1)} %param.7) | copy-start | bytes 6291460
  6.5 272.4 %reduce-scatter.2.cloned.1.call-start = ((), (), s32[]{:S(2)}) async-start(), calls=%async_computation.1 | async-start | bytes 13369344 | tf_op jit(solution)/shard_map/reduce_scatter | solution.py:68
  25.4 7.8 %copy-start.2 = (f32[256]{0:T(256)}, f32[256]{0:T(256)S(1)}, u32[]{:S(2)}) copy-start(f32[256]{0:T(256)S(1)} %get-tuple-element.28) | copy-start | bytes 3076
  33.2 0.6 copy-start.4
  33.2 0.6 copy-start.5
  135.8 3.9 %copy-start.1 = (bf16[2,256,3072]{2,1,0:T(8,128)(2,1)S(1)}, bf16[2,256,3072]{2,1,0:T(8,128)(2,1)}, u32[]{:S(2)}) copy-start(bf16[2,256,3072]{2,1,0:T(8,128)(2,1)} %param.4) | copy-start | bytes 9437188
  135.8 3.9 %copy-start.3 = (f32[256]{0:T(256)S(1)}, f32[256]{0:T(256)}, u32[]{:S(2)}) copy-start(f32[256]{0:T(256)} %copy-done.2) | copy-start | bytes 3076
Sparse Core Ops, SparseCore 0:
  146.7 132.1 reduce-scatter.1
